TPU v7x, 256 devices: a whole 4x4x8 slice. The times are simulated.
256 devices in a mesh: dp: 2 (over z_hi), tensor: 4 (over y), pool: 32 (over x, z_lo, core).
Axes of the slice: x: 4, y: 4, z: 8 (z_hi: 2, z_lo: 4; z = z_hi * 4 + z_lo), core: 2. Of those that a mesh axis runs over, the one named last changes fastest.
Arguments:
- tokens: bfloat16 [64, 1024, 4096], P(('dp', 'pool')), may hold values from -192 to 192, as said below
- w_hidden: bfloat16 [4096, 4096], P('pool', 'tensor'), may hold values from -0.09375 to 0.09375
- w_out: bfloat16 [4096, 256], P('tensor'), may hold values from -0.09375 to 0.09375
- bank: bfloat16 [32768, 256], P('pool'), may hold values from -0.5 to 0.5
- item_ids: int32 [32768], P('pool'), may hold values from 0 to 1048575
- log_freq: bfloat16 [1048576], replicated, may hold values from -14 to -6
- positives: int32 [64, 1024], P(('dp', 'pool'), 'tensor'), may hold values from 0 to 32767
- new_items: bfloat16 [8192, 256], P('pool'), may hold values from -0.5 to 0.5
- new_owner: int32 [8192, 1], P('pool'), may hold values from 0 to 31; in each aligned block of 256 rows (0 to 255, 256 to 511, ...) at most 16 rows name the same one
- queue_head: int32 [32], P('pool'), may hold values from 0 to 1023
Outputs:
- query_loss: float32 [64, 1024], P(('dp', 'pool'), 'tensor')
- new_bank: bfloat16 [32768, 256], P('pool')
Inputs may be any that keep to these rules, and one draw needn't show every extreme that they name: `tokens`: float values within the range. `new_owner`: among the 256 new rows of one pool index, no shard is named by more than 16 rows, a bound that some block reaches.
All inputs are finite; a program needn't handle non-finite values.
Results may differ from a plain program's by a relative error of at most 0.002.
Values may be sent and summed in bfloat16 or wider, within the bound.
A program may use at most 128 MiB of HBM per device.

v0:
```python
import jax
import jax.numpy as jnp
from jax import lax
from jax.sharding import Mesh
from jax.sharding import PartitionSpec as P

POOL = ("pool_0", "pool_1", "pool_2")
DP_POOL = ("dp", "pool_0", "pool_1", "pool_2")
inv_temp = 5.0


def split_up(x, dim, count):
    before, after = (x.shape[:dim], x.shape[dim + 1 :])
    return jnp.moveaxis(x.reshape(*before, count, -1, *after), dim, 0)


def sum_at_owner(x, axis, dim):
    count = lax.axis_size(axis)
    blocks = lax.all_to_all(split_up(x, dim, count), axis, 0, 0, tiled=True)
    return jnp.sum(blocks, axis=0)


def all_in_one(x, axis):
    leaves = jax.tree.leaves(x)
    turns = sorted(range(len(leaves)), key=lambda k: -leaves[k].size)
    width = (1, *leaves[turns[0]].shape)[-1]
    lines = [
        jnp.pad(leaves[k].reshape(-1), (0, -leaves[k].size % width)).reshape(-1, width)
        for k in turns
    ]
    both, at, found = (lax.all_gather(jnp.concatenate(lines), axis), 0, {})
    for k, line in zip(turns, lines):
        section = both[:, at : at + len(line)].reshape(len(both), -1)
        found[k] = section[:, : leaves[k].size].reshape(-1, *leaves[k].shape)
        at += len(line)
    numbers = iter(range(len(leaves)))
    return jax.tree.map(lambda _: found[next(numbers)], x)


def joined_all(x, axes, combine):
    for axis in axes:
        pieces = all_in_one(x, axis)
        x = jax.tree.map(lambda part: part[0], pieces)
        for k in range(1, lax.axis_size(axis)):
            x = combine(x, jax.tree.map(lambda part: part[k], pieces))
    return x


def copy_for_each(x, axis):
    copies = jnp.broadcast_to(x, (lax.axis_size(axis), *x.shape))
    return lax.all_to_all(copies, axis, split_axis=0, concat_axis=0, tiled=True)


def folded_in_pairs(pieces, combine):
    while len(jax.tree.leaves(pieces)[0]) > 1:
        pieces = jax.vmap(combine)(*(pieces[side::2] for side in (0, 1)))
    return pieces[0]


def entering(x, axis, combine, identity):
    count, position = (lax.axis_size(axis), lax.axis_index(axis))
    passed = jnp.arange(count) < position

    def kept(part, zero, own):
        part = jnp.where(
            passed.reshape(-1, *(1 for _ in own.shape)), part, jnp.asarray(zero, own.dtype)
        )
        return part

    pieces = copy_for_each(x, axis)
    return folded_in_pairs(kept(pieces, identity, x), combine)


def local_stats(query_rows, target_rows, bank, offsets, base_column):
    row_count = query_rows.shape[0]
    bank_rows = bank.shape[0]
    block_width = 512
    block_count = bank_rows // block_width
    blocks = bank.reshape(block_count, block_width, bank.shape[1])
    shifts = offsets.reshape(block_count, block_width)

    def block_step(running, inputs):
        run_max, run_sum, run_pos = running
        bank_block, block_offsets, block_index = inputs
        logits = (
            inv_temp * jnp.dot(query_rows, bank_block.T, preferred_element_type=jnp.float32)
            - block_offsets[None, :]
        )
        next_max = jnp.maximum(run_max, jnp.max(logits, axis=1))
        run_sum = run_sum * jnp.exp(run_max - next_max) + jnp.sum(
            jnp.exp(logits - next_max[:, None]), axis=1
        )
        columns = base_column + block_index * block_width + jnp.arange(block_width, dtype=jnp.int32)
        run_pos = run_pos + jnp.sum(
            jnp.where(columns[None, :] == target_rows[:, None], logits, 0.0), axis=1
        )
        return ((next_max, run_sum, run_pos), None)

    initial = (
        jnp.full((row_count,), -jnp.inf, jnp.float32),
        jnp.zeros((row_count,), jnp.float32),
        jnp.zeros((row_count,), jnp.float32),
    )
    final, _ = lax.scan(
        block_step, initial, (blocks, shifts, jnp.arange(block_count, dtype=jnp.int32))
    )
    return final


def combine(earlier_part, later_part):
    both_max = jnp.maximum(earlier_part[0], later_part[0])
    both_sum = earlier_part[1] * jnp.exp(earlier_part[0] - both_max) + later_part[1] * jnp.exp(
        later_part[0] - both_max
    )
    return (both_max, both_sum, earlier_part[2] + later_part[2])


def add_counts(earlier_part, later_part):
    return earlier_part + later_part


def body(
    tokens, w_hidden, w_out, bank, item_ids, log_freq, positives, new_items, new_owner, queue_head
):
    token_rows = tokens[0]
    pre_act = jnp.dot(
        token_rows,
        lax.all_gather(w_hidden, POOL, axis=0, tiled=True),
        preferred_element_type=jnp.float32,
    )
    hidden = jnp.maximum(pre_act, 0.0).astype(jnp.bfloat16)
    partial_value = jnp.dot(hidden, w_out, preferred_element_type=jnp.float32)
    queries = sum_at_owner(partial_value, "tensor", 0).astype(jnp.bfloat16)
    offsets = jnp.take(log_freq, item_ids).astype(jnp.float32)
    own_index = lax.axis_index(POOL)
    base_column = own_index * bank.shape[0]
    query_piece = lax.all_gather(queries[None], POOL, axis=0, tiled=True)
    target_piece = lax.all_gather(positives, POOL, axis=0, tiled=True)
    groups_in = query_piece.shape[0]
    run_max, run_sum, run_pos = local_stats(
        query_piece.reshape(-1, query_piece.shape[2]),
        target_piece.reshape(-1),
        bank,
        offsets,
        base_column,
    )
    maxima = run_max.reshape(groups_in, -1)
    totals = run_sum.reshape(groups_in, -1)
    scores = run_pos.reshape(groups_in, -1)
    maxima, totals, scores = (maxima, totals, scores)
    maxima, totals, scores = joined_all((maxima, totals, scores), POOL, combine)
    own_max = lax.dynamic_slice_in_dim(maxima, own_index, 1, 0)
    own_sum = lax.dynamic_slice_in_dim(totals, own_index, 1, 0)
    own_pos = lax.dynamic_slice_in_dim(scores, own_index, 1, 0)
    query_loss = own_max + jnp.log(own_sum) - own_pos
    owners = new_owner[:, 0]
    head_slot = queue_head[0]
    shard_rows = bank.shape[0]
    peer_count = lax.axis_size(POOL)
    local_rows = new_items.shape[0]
    capacity = 2 * local_rows // peer_count
    onehot = (owners[:, None] == jnp.arange(peer_count, dtype=jnp.int32)[None, :]).astype(jnp.int32)
    counts = jnp.sum(onehot, axis=0, dtype=jnp.int32)
    before = jnp.sum(
        (jnp.cumsum(onehot, axis=0, dtype=jnp.int32) - onehot) * onehot, axis=1, dtype=jnp.int32
    )
    earlier = entering(counts, POOL, add_counts, jnp.zeros_like(counts))
    ranks = before + jnp.sum(onehot * earlier[None, :], axis=1, dtype=jnp.int32)
    send_pos = owners * capacity + before
    rows_out = (
        jnp.zeros((peer_count * capacity, new_items.shape[1]), jnp.bfloat16)
        .at[send_pos]
        .set(new_items)
    )
    ranks_out = jnp.full((peer_count * capacity,), -1, jnp.int32).at[send_pos].set(ranks)
    rows_in, ranks_in = (
        lax.all_to_all(
            rows_out.reshape(peer_count, capacity, -1),
            POOL,
            split_axis=0,
            concat_axis=0,
            tiled=True,
        ),
        lax.all_to_all(
            ranks_out.reshape(peer_count, capacity), POOL, split_axis=0, concat_axis=0, tiled=True
        ),
    )
    local_slots = jnp.where(ranks_in >= 0, (head_slot + ranks_in) % shard_rows, shard_rows).reshape(
        -1
    )
    new_bank = bank.at[local_slots].set(rows_in.reshape(-1, new_items.shape[1]), mode="drop")
    return (query_loss, new_bank)


def solution(mesh):
    finer = Mesh(
        mesh.devices.reshape(mesh.shape["dp"], mesh.shape["tensor"], 4, 4, 2),
        ("dp", "tensor", "pool_0", "pool_1", "pool_2"),
    )
    in_specs = (
        P(DP_POOL, None, None),
        P(POOL, "tensor"),
        P("tensor", None),
        P(POOL, None),
        P(POOL),
        P(),
        P(DP_POOL, "tensor"),
        P(POOL, None),
        P(POOL, None),
        P(POOL),
    )
    out_specs = (P(DP_POOL, "tensor"), P(POOL, None))
    return jax.shard_map(body, mesh=finer, in_specs=in_specs, out_specs=out_specs, check_vma=False)
```

profile of v0, /device:TPU:1, one launch (start us, length us, event | category | flops | bytes accessed | tf_op | source)
XLA Modules:
  0.0 274.3 jit_solution(2599973721477552642)
XLA Ops:
  7.2 0.7 all-gather.8.cloned.1.call-update
  8.0 74.6 %all-gather.8.cloned.1.call-done = bf16[4096,1024]{1,0:T(8,128)(2,1)} async-done(((bf16[128,1024]{1,0:T(8,128)(2,1)}), bf16[4096,1024]{1,0:T(8,128)(2,1)}) %all-gather.8.cloned.1.call-update) | async-done | bytes 8388624 | tf_op jit(solution)/shard_map/all_gather | solution.py:128
  82.6 16.4 %fusion.12 = f32[1024,256]{1,0:T(8,128)} fusion(bf16[1024,256]{1,0:T(8,128)(2,1)} %param.14, bf16[4096,1024]{1,0:T(8,128)(2,1)} %all-gather.8.cloned.1.call-done, bf16[1,1024,4096]{2,1,0:T(8,128)(2,1)} %param.12), kind=kOutput, calls=%fused_computation.22 | convolution fusion | flops 9128902656 | bytes 18350080 | tf_op jit(solution)/shard_map/dot_general | solution.py:132
  98.9 19.1 %all_to_all.28 = f32[4,256,256]{2,1,0:T(8,128)} all-to-all(f32[4,256,256]{2,1,0:T(8,128)} %bitcast.252), channel_id=1, replica_groups=mesh['dp'=2,'tensor'=4,'pool_0'=4,'pool_1'=4,'pool_2'=2] {'tensor'}, dimensions={0} | all-to-all | bytes 2097152 | tf_op jit(solution)/shard_map/all_to_all | solution.py:19
  118.0 2.0 reduce_sum.56
  120.2 0.6 broadcast_in_dim.52
  120.8 6.5 %all-to-all-start.1 = ((s32[32,1,32]{2,1,0:T(1,128)}), s32[32,1,32]{2,1,0:T(1,128)S(1)}, u32[]{:S(2)}, u32[]{:S(2)}) async-start(s32[32,1,32]{2,1,0:T(1,128)} %broadcast_in_dim.52), calls=%async_computation.1 | async-start | bytes 32768 | tf_op jit(solution)/shard_map/all_to_all | solution.py:51
  127.3 6.8 %gather_fusion = bf16[1024]{0:T(1024)(128)(2,1)S(1)} fusion(bf16[1048576]{0:T(1024)(128)(2,1)S(1)} %copy-done, s32[1024]{0:T(1024)S(1)} %fusion.46), kind=kCustom, calls=%fused_computation | custom fusion | bytes 8192 | tf_op jit(solution)/shard_map/jit(_take)/gather | solution.py:134
  135.4 1.4 scatter_custom_fusion
  136.8 0.7 all_to_all.21
  137.5 7.7 %all-to-all-start.2 = ((s32[32,1,16]{2,1,0:T(1,128)}), s32[32,1,16]{2,1,0:T(1,128)S(1)}, u32[]{:S(2)}, u32[]{:S(2)}) async-start(s32[32,1,16]{2,1,0:T(1,128)} %bitcast.37), calls=%async_computation.2 | async-start | bytes 32768 | tf_op jit(solution)/shard_map/all_to_all | solution.py:184
  145.2 43.7 %all-gather.4 = s32[32,1,256]{2,1,0:T(1,128)S(1)} all-gather(s32[1,1,256]{2,1,0:T(1,128)S(1)} %bitcast.259), channel_id=1, replica_groups=mesh['dp'=2,'tensor'=4,'pool_0'=4,'pool_1'=4,'pool_2'=2] {'pool_0','pool..., dimensions={0}, use_global_device_ids=true | all-gather | bytes 33792 | tf_op jit(solution)/shard_map/all_gather | solution.py:138
  189.6 2.5 scatter_custom_fusion.1
  192.1 3.7 %all-to-all-start.3 = ((bf16[32,16,256]{2,1,0:T(8,128)(2,1)}), bf16[32,16,256]{2,1,0:T(8,128)(2,1)S(1)}, u32[]{:S(2)}, u32[]{:S(2)}) async-start(bf16[32,16,256]{2,1,0:T(8,128)(2,1)} %bitcast.40), calls=%async_computation.3 | async-start | bytes 524288 | tf_op jit(solution)/shard_map/all_to_all | solution.py:177
  196.1 37.4 %while.15 = (s32[]{:T(128)}, f32[8192]{0:T(1024)S(1)}, f32[8192]{0:T(1024)S(1)}, f32[8192]{0:T(1024)S(1)}, bf16[2,512,256]{2,1,0:T(8,128)(2,1)S(1)}, /*index=5*/...) while((s32[]{:T(128)}, f32[8192]{0:T(1024)S(1)}, ...), condition=%wide.region_5.6_spmd.clone, body=%wide.region_1.5_spmd.clone.sunk | while | flops 2181087744 | bytes 38676668 | solution.py:104
  196.2 9.2 %fusion.74 = (f32[8192]{0:T(1024)S(1)}, f32[512,8192]{1,0:T(8,128)}) fusion(f32[512]{0:T(512)S(1)} %bitcast.241, bf16[8192,256]{1,0:T(8,128)(2,1)} %get-tuple-element.234, bf16[2,512,256]{2,1,0:T(8,128)(2,1)S(1)} %get-tuple-element.233, s32[]{:T(128)S(6)} %copy.27), kind=kOutput, calls=%fused_computation.130.clone.1 | convolution fusion | flops 2160058368 | bytes 21268484 | tf_op jit(solution)/shard_map/while/body/eval_jaxpr/dot_general | solution.py:86
  206.7 8.1 %fusion.75 = (f32[8192]{0:T(1024)S(1)}, f32[8192]{0:T(1024)S(1)}) fusion(f32[512,8192]{1,0:T(8,128)} %get-tuple-element.198, s32[8192]{0:T(1024)S(1)} %bitcast.242, s32[512]{0:T(512)S(1)} %iota_add_fusion.2, f32[8192]{0:T(1024)S(1)} %select_maximum_fusion.2), kind=kLoop, calls=%fused_computation.8.clone.1 | loop fusion | flops 20955136 | bytes 16910336 | tf_op jit(solution)/shard_map/while/body/eval_jaxpr/reduce_sum | solution.py:94
  214.8 9.2 %fusion.74 = (f32[8192]{0:T(1024)S(1)}, f32[512,8192]{1,0:T(8,128)}) fusion(f32[512]{0:T(512)S(1)} %bitcast.241, bf16[8192,256]{1,0:T(8,128)(2,1)} %get-tuple-element.234, bf16[2,512,256]{2,1,0:T(8,128)(2,1)S(1)} %get-tuple-element.233, s32[]{:T(128)S(6)} %copy.27), kind=kOutput, calls=%fused_computation.130.clone.1 | convolution fusion | flops 2160058368 | bytes 21268484 | tf_op jit(solution)/shard_map/while/body/eval_jaxpr/dot_general | solution.py:86
  225.3 8.1 %fusion.75 = (f32[8192]{0:T(1024)S(1)}, f32[8192]{0:T(1024)S(1)}) fusion(f32[512,8192]{1,0:T(8,128)} %get-tuple-element.198, s32[8192]{0:T(1024)S(1)} %bitcast.242, s32[512]{0:T(512)S(1)} %iota_add_fusion.2, f32[8192]{0:T(1024)S(1)} %select_maximum_fusion.2), kind=kLoop, calls=%fused_computation.8.clone.1 | loop fusion | flops 20955136 | bytes 16910336 | tf_op jit(solution)/shard_map/while/body/eval_jaxpr/reduce_sum | solution.py:94
  233.6 10.9 %all-gather.1 = f32[384,256]{1,0:T(8,128)S(1)} all-gather(f32[96,256]{1,0:T(8,128)S(1)} %pad_maximum_fusion), channel_id=3, replica_groups=mesh['dp'=2,'tensor'=4,'pool_0'=4,'pool_1'=4,'pool_2'=2] {'pool_0'}, dimensions={0}, use_global_device_ids=true | all-gather | bytes 491520 | tf_op jit(solution)/shard_map/all_gather | solution.py:31
  244.6 11.7 %all-gather.2 = f32[384,256]{1,0:T(8,128)S(1)} all-gather(f32[96,256]{1,0:T(8,128)S(1)} %pad_maximum_fusion.1), channel_id=4, replica_groups=mesh['dp'=2,'tensor'=4,'pool_0'=4,'pool_1'=4,'pool_2'=2] {'pool_1'}, dimensions={0}, use_global_device_ids=true | all-gather | bytes 491520 | tf_op jit(solution)/shard_map/all_gather | solution.py:31
  256.3 7.7 %all-gather.3 = f32[192,256]{1,0:T(8,128)S(1)} all-gather(f32[96,256]{1,0:T(8,128)S(1)} %pad_maximum_fusion.2), channel_id=5, replica_groups=mesh['dp'=2,'tensor'=4,'pool_0'=4,'pool_1'=4,'pool_2'=2] {'pool_2'}, dimensions={0}, use_global_device_ids=true | all-gather | bytes 294912 | tf_op jit(solution)/shard_map/all_gather | solution.py:31
  264.1 2.6 scatter_fusion
  266.7 0.7 fusion.54
  (82 shorter events, 3.4 us)
Async XLA Ops:
  7.2 120.1 %copy-start = (bf16[1048576]{0:T(1024)(128)(2,1)S(1)}, bf16[1048576]{0:T(1024)(128)(2,1)}, u32[]{:S(2)}) copy-start(bf16[1048576]{0:T(1024)(128)(2,1)} %param.17) | copy-start | bytes 6291460
  7.2 75.4 %all-gather.8.cloned.1.call-start = ((), (), s32[]{:S(2)}) async-start(), calls=%async_computation.4 | async-start | bytes 8650752 | tf_op jit(solution)/shard_map/all_gather | solution.py:128
  7.9 112.1 %copy-start.4 = (s32[256,1]{0,1:T(1,128)S(1)}, s32[256,1]{0,1:T(1,128)}, u32[]{:S(2)}) copy-start(s32[256,1]{0,1:T(1,128)} %param.20) | copy-start | bytes 3076
  7.9 119.3 %copy-start.3 = (s32[1024]{0:T(1024)S(1)}, s32[1024]{0:T(1024)}, u32[]{:S(2)}) copy-start(s32[1024]{0:T(1024)} %param.16) | copy-start | bytes 12292
  7.9 137.2 %copy-start.5 = (s32[1,256]{1,0:T(1,128)S(1)}, s32[1,256]{1,0:T(1,128)}, u32[]{:S(2)}) copy-start(s32[1,256]{1,0:T(1,128)} %param.18) | copy-start | bytes 3076
  7.9 188.2 %copy-start.2 = (bf16[1024,256]{1,0:T(8,128)(2,1)S(1)}, bf16[1024,256]{1,0:T(8,128)(2,1)}, u32[]{:S(2)}) copy-start(bf16[1024,256]{1,0:T(8,128)(2,1)} %param.15) | copy-start | bytes 1572868
  8.0 188.2 %all-gather.10.cloned.1.call-start = ((), (), s32[]{:S(2)}) async-start(), calls=%async_computation.5 | async-start | bytes 4325376 | tf_op jit(solution)/shard_map/all_gather | solution.py:137
  120.8 14.2 %all-to-all-start.1 = ((s32[32,1,32]{2,1,0:T(1,128)}), s32[32,1,32]{2,1,0:T(1,128)S(1)}, u32[]{:S(2)}, u32[]{:S(2)}) async-start(s32[32,1,32]{2,1,0:T(1,128)} %broadcast_in_dim.52), calls=%async_computation.1 | async-start | bytes 32768 | tf_op jit(solution)/shard_map/all_to_all | solution.py:51
  137.5 54.6 %all-to-all-start.2 = ((s32[32,1,16]{2,1,0:T(1,128)}), s32[32,1,16]{2,1,0:T(1,128)S(1)}, u32[]{:S(2)}, u32[]{:S(2)}) async-start(s32[32,1,16]{2,1,0:T(1,128)} %bitcast.37), calls=%async_computation.2 | async-start | bytes 32768 | tf_op jit(solution)/shard_map/all_to_all | solution.py:184
  192.1 72.0 %all-to-all-start.3 = ((bf16[32,16,256]{2,1,0:T(8,128)(2,1)}), bf16[32,16,256]{2,1,0:T(8,128)(2,1)S(1)}, u32[]{:S(2)}, u32[]{:S(2)}) async-start(bf16[32,16,256]{2,1,0:T(8,128)(2,1)} %bitcast.40), calls=%async_computation.3 | async-start | bytes 524288 | tf_op jit(solution)/shard_map/all_to_all | solution.py:177
  266.7 0.8 copy-start.1
Sparse Core Ops, SparseCore 0:
  9.8 72.6 all-gather.7
  120.2 60.7 all-gather.9
where the time goes:
time: 275 us; the launch traced here: 274 us
  blocking collectives  93.1 us (34%)
  waiting for transfers between devices  75.3 us (27%)
  matrix products  34.8 us (13%)
  other arithmetic  20.1 us (7%)
  starting transfers between devices  17.9 us (7%)
  local copies, waits for them, and re-layouts  16.6 us (6%)
  between operations  15 us (5%)
    all_gather x1, waiting for transfers between devices, body(): lax.all_gather(w_hidden, POOL, axis=0, tiled=True)  74.6 us
    all_gather x1, blocking collectives, body(): target_piece = lax.all_gather(positives, POOL, axis=0, tiled=True)  43.7 us
    all_gather x3, blocking collectives, all_in_one(): both, at, found = (lax.all_gather(jnp.concatenate(lines), axis), 0, {})  30.3 us
    all_to_all x1, blocking collectives, sum_at_owner(): blocks = lax.all_to_all(split_up(x, dim, count), axis, 0, 0, tiled=True)  19.1 us
    dot_general x2, matrix products, block_step(): jnp.dot(query_rows, bank_block.T, preferred_element_type=jnp.float32)  18.5 us
    dot_general x1, matrix products, body(): partial_value = jnp.dot(hidden, w_out, preferred_element_type=jnp.float32)  16.4 us
    reduce_sum x2, other arithmetic, block_step(): jnp.sum(jnp.where(columns[None, :] == target_rows[:, None], logits, 0.0),...  16.2 us
    all_to_all x1, starting transfers between devices, body(): lax.all_to_all(ranks_out.reshape(peer_count, capacity), POOL, split_axis=...  7.69 us
  transfers between devices with their start and end apart: 5, of which 1 were waited for; matrix products, arithmetic and copies ran while one was open for 18% of the time, Pallas kernels for 0%

commit v1 on v0

--- a/solution.py
+++ b/solution.py
@@ -125,7 +125,9 @@
     token_rows = tokens[0]
     pre_act = jnp.dot(
         token_rows,
-        lax.all_gather(w_hidden, POOL, axis=0, tiled=True),
+        jnp.concatenate(
+            lax.all_to_all(jnp.stack([w_hidden] * lax.axis_size(POOL)), POOL, 0, 0), axis=0
+        ),
         preferred_element_type=jnp.float32,
     )
     hidden = jnp.maximum(pre_act, 0.0).astype(jnp.bfloat16)

time: 275 us -> 395 us (1.44)
  blocking collectives: 93.1 us -> 288 us
  waiting for transfers between devices: 75.3 us -> 0.04 us
    all_to_all x0 -> x1, blocking collectives: none -> 195 us  [body(): lax.all_to_all(jnp.stack([w_hidden] * lax.axis_size(POOL)), POOL, 0, 0)]
    all_gather x1 -> x0, waiting for transfers between devices: 74.6 us -> none  [body(): lax.all_gather(w_hidden, POOL, axis=0, tiled=True)]
  transfers between devices with their start and end apart: 5 -> 4, of which waited for: 1 -> 0; matrix products, arithmetic and copies ran while one was open for 18% -> 12% of each run, Pallas kernels for 0% -> 0%
where the time goes in v1:
time: 395 us
  blocking collectives  288 us (73%)
  matrix products  34.8 us (9%)
  other arithmetic  20.1 us (5%)
  local copies, waits for them, and re-layouts  18.8 us (5%)
  starting transfers between devices  16.4 us (4%)
  between operations  15 us (4%)
    all_to_all x1, blocking collectives, body(): lax.all_to_all(jnp.stack([w_hidden] * lax.axis_size(POOL)), POOL, 0, 0)  195 us
    all_gather x1, blocking collectives, body(): target_piece = lax.all_gather(positives, POOL, axis=0, tiled=True)  43.7 us
    all_gather x3, blocking collectives, all_in_one(): both, at, found = (lax.all_gather(jnp.concatenate(lines), axis), 0, {})  30.3 us
    all_to_all x1, blocking collectives, sum_at_owner(): blocks = lax.all_to_all(split_up(x, dim, count), axis, 0, 0, tiled=True)  19 us
    dot_general x2, matrix products, block_step(): jnp.dot(query_rows, bank_block.T, preferred_element_type=jnp.float32)  18.5 us
    dot_general x1, matrix products, body(): partial_value = jnp.dot(hidden, w_out, preferred_element_type=jnp.float32)  16.4 us
    reduce_sum x2, other arithmetic, block_step(): jnp.sum(jnp.where(columns[None, :] == target_rows[:, None], logits, 0.0),...  16.2 us
  transfers between devices with their start and end apart: 4, of which 0 were waited for; matrix products, arithmetic and copies ran while one was open for 12% of the time, Pallas kernels for 0%

profile of v1, /device:TPU:1, one launch (start us, length us, event | category | flops | bytes accessed | tf_op | source)
XLA Modules:
  0.0 394.7 jit_solution(17531096805542949611)
XLA Ops:
  7.2 2.2 stack.2
  9.4 195.2 %all_to_all.33 = bf16[32,128,1024]{2,1,0:T(8,128)(2,1)} all-to-all(bf16[32,128,1024]{2,1,0:T(8,128)(2,1)S(1)} %stack.2), channel_id=1, replica_groups=mesh['dp'=2,'tensor'=4,'pool_0'=4,'pool_1'=4,'pool_2'=2] {'pool_0','pool..., dimensions={0} | all-to-all | bytes 16777216 | tf_op jit(solution)/shard_map/all_to_all | solution.py:129
  204.6 16.4 %fusion.12 = f32[1024,256]{1,0:T(8,128)} fusion(bf16[1024,256]{1,0:T(8,128)(2,1)S(1)} %copy-done.6, bf16[4096,1024]{1,0:T(8,128)(2,1)} %bitcast.242, bf16[1,1024,4096]{2,1,0:T(8,128)(2,1)} %param.12), kind=kOutput, calls=%fused_computation.22 | convolution fusion | flops 9128902656 | bytes 18350080 | tf_op jit(solution)/shard_map/dot_general | solution.py:134
  221.0 19.0 %all_to_all.34 = f32[4,256,256]{2,1,0:T(8,128)} all-to-all(f32[4,256,256]{2,1,0:T(8,128)} %bitcast.254), channel_id=1, replica_groups=mesh['dp'=2,'tensor'=4,'pool_0'=4,'pool_1'=4,'pool_2'=2] {'tensor'}, dimensions={0} | all-to-all | bytes 2097152 | tf_op jit(solution)/shard_map/all_to_all | solution.py:19
  240.0 2.0 reduce_sum.56
  242.1 0.6 broadcast_in_dim.52
  242.7 4.8 %all-to-all-start.2 = ((s32[32,1,32]{2,1,0:T(1,128)}), s32[32,1,32]{2,1,0:T(1,128)S(1)}, u32[]{:S(2)}, u32[]{:S(2)}) async-start(s32[32,1,32]{2,1,0:T(1,128)} %broadcast_in_dim.52), calls=%async_computation.2 | async-start | bytes 32768 | tf_op jit(solution)/shard_map/all_to_all | solution.py:51
  247.6 6.8 %gather_fusion = bf16[1024]{0:T(1024)(128)(2,1)S(1)} fusion(bf16[1048576]{0:T(1024)(128)(2,1)S(1)} %copy-done, s32[1024]{0:T(1024)S(1)} %fusion.46), kind=kCustom, calls=%fused_computation | custom fusion | bytes 8192 | tf_op jit(solution)/shard_map/jit(_take)/gather | solution.py:136
  255.7 1.4 scatter_custom_fusion
  257.1 0.7 all_to_all.25
  257.8 7.8 %all-to-all-start.3 = ((s32[32,1,16]{2,1,0:T(1,128)}), s32[32,1,16]{2,1,0:T(1,128)S(1)}, u32[]{:S(2)}, u32[]{:S(2)}) async-start(s32[32,1,16]{2,1,0:T(1,128)} %bitcast.38), calls=%async_computation.3 | async-start | bytes 32768 | tf_op jit(solution)/shard_map/all_to_all | solution.py:186
  265.6 43.7 %all-gather.4 = s32[32,1,256]{2,1,0:T(1,128)S(1)} all-gather(s32[1,1,256]{2,1,0:T(1,128)S(1)} %bitcast.261), channel_id=1, replica_groups=mesh['dp'=2,'tensor'=4,'pool_0'=4,'pool_1'=4,'pool_2'=2] {'pool_0','pool..., dimensions={0}, use_global_device_ids=true | all-gather | bytes 33792 | tf_op jit(solution)/shard_map/all_gather | solution.py:140
  309.9 2.5 scatter_custom_fusion.1
  312.5 3.7 all-to-all-start.4
  316.5 37.3 %while.15 = (s32[]{:T(128)}, f32[8192]{0:T(1024)S(1)}, f32[8192]{0:T(1024)S(1)}, f32[8192]{0:T(1024)S(1)}, bf16[2,512,256]{2,1,0:T(8,128)(2,1)S(1)}, /*index=5*/...) while((s32[]{:T(128)}, f32[8192]{0:T(1024)S(1)}, ...), condition=%wide.region_5.6_spmd.clone, body=%wide.region_1.5_spmd.clone.sunk | while | flops 2181087744 | bytes 38676660 | solution.py:104
  316.6 9.2 %fusion.74 = (f32[8192]{0:T(1024)S(1)}, f32[512,8192]{1,0:T(8,128)}) fusion(f32[512]{0:T(512)S(1)} %bitcast.243, bf16[8192,256]{1,0:T(8,128)(2,1)} %get-tuple-element.234, bf16[2,512,256]{2,1,0:T(8,128)(2,1)S(1)} %get-tuple-element.233, s32[]{:T(128)} %get-tuple-element.216), kind=kOutput, calls=%fused_computation.130.clone.1 | convolution fusion | flops 2160058368 | bytes 21268484 | tf_op jit(solution)/shard_map/while/body/eval_jaxpr/dot_general | solution.py:86
  327.0 8.1 %fusion.75 = (f32[8192]{0:T(1024)S(1)}, f32[8192]{0:T(1024)S(1)}) fusion(f32[512,8192]{1,0:T(8,128)} %get-tuple-element.198, s32[8192]{0:T(1024)S(1)} %bitcast.244, s32[512]{0:T(512)S(1)} %iota_add_fusion.2, f32[8192]{0:T(1024)S(1)} %select_maximum_fusion.2), kind=kLoop, calls=%fused_computation.8.clone.1 | loop fusion | flops 20955136 | bytes 16910336 | tf_op jit(solution)/shard_map/while/body/eval_jaxpr/reduce_sum | solution.py:94
  335.2 9.2 %fusion.74 = (f32[8192]{0:T(1024)S(1)}, f32[512,8192]{1,0:T(8,128)}) fusion(f32[512]{0:T(512)S(1)} %bitcast.243, bf16[8192,256]{1,0:T(8,128)(2,1)} %get-tuple-element.234, bf16[2,512,256]{2,1,0:T(8,128)(2,1)S(1)} %get-tuple-element.233, s32[]{:T(128)} %get-tuple-element.216), kind=kOutput, calls=%fused_computation.130.clone.1 | convolution fusion | flops 2160058368 | bytes 21268484 | tf_op jit(solution)/shard_map/while/body/eval_jaxpr/dot_general | solution.py:86
  345.7 8.1 %fusion.75 = (f32[8192]{0:T(1024)S(1)}, f32[8192]{0:T(1024)S(1)}) fusion(f32[512,8192]{1,0:T(8,128)} %get-tuple-element.198, s32[8192]{0:T(1024)S(1)} %bitcast.244, s32[512]{0:T(512)S(1)} %iota_add_fusion.2, f32[8192]{0:T(1024)S(1)} %select_maximum_fusion.2), kind=kLoop, calls=%fused_computation.8.clone.1 | loop fusion | flops 20955136 | bytes 16910336 | tf_op jit(solution)/shard_map/while/body/eval_jaxpr/reduce_sum | solution.py:94
  353.9 10.9 %all-gather.1 = f32[384,256]{1,0:T(8,128)S(1)} all-gather(f32[96,256]{1,0:T(8,128)S(1)} %pad_maximum_fusion), channel_id=3, replica_groups=mesh['dp'=2,'tensor'=4,'pool_0'=4,'pool_1'=4,'pool_2'=2] {'pool_0'}, dimensions={0}, use_global_device_ids=true | all-gather | bytes 491520 | tf_op jit(solution)/shard_map/all_gather | solution.py:31
  364.9 11.7 %all-gather.2 = f32[384,256]{1,0:T(8,128)S(1)} all-gather(f32[96,256]{1,0:T(8,128)S(1)} %pad_maximum_fusion.1), channel_id=4, replica_groups=mesh['dp'=2,'tensor'=4,'pool_0'=4,'pool_1'=4,'pool_2'=2] {'pool_1'}, dimensions={0}, use_global_device_ids=true | all-gather | bytes 491520 | tf_op jit(solution)/shard_map/all_gather | solution.py:31
  376.7 7.7 %all-gather.3 = f32[192,256]{1,0:T(8,128)S(1)} all-gather(f32[96,256]{1,0:T(8,128)S(1)} %pad_maximum_fusion.2), channel_id=5, replica_groups=mesh['dp'=2,'tensor'=4,'pool_0'=4,'pool_1'=4,'pool_2'=2] {'pool_2'}, dimensions={0}, use_global_device_ids=true | all-gather | bytes 294912 | tf_op jit(solution)/shard_map/all_gather | solution.py:31
  384.4 2.6 scatter_fusion
  387.0 0.7 fusion.54
  (83 shorter events, 3.4 us)
Async XLA Ops:
  7.2 240.4 %copy-start = (bf16[1048576]{0:T(1024)(128)(2,1)S(1)}, bf16[1048576]{0:T(1024)(128)(2,1)}, u32[]{:S(2)}) copy-start(bf16[1048576]{0:T(1024)(128)(2,1)} %param.17) | copy-start | bytes 6291460
  7.2 309.3 %all-gather.7.cloned.1.call-start = ((), (), s32[]{:S(2)}) async-start(), calls=%async_computation.5 | async-start | bytes 4325376 | tf_op jit(solution)/shard_map/all_gather | solution.py:139
  9.4 195.2 %copy-start.6 = (bf16[1024,256]{1,0:T(8,128)(2,1)S(1)}, bf16[1024,256]{1,0:T(8,128)(2,1)}, u32[]{:S(2)}) copy-start(bf16[1024,256]{1,0:T(8,128)(2,1)} %param.14) | copy-start | bytes 1572868
  204.6 37.4 %copy-start.4 = (s32[256,1]{0,1:T(1,128)S(1)}, s32[256,1]{0,1:T(1,128)}, u32[]{:S(2)}) copy-start(s32[256,1]{0,1:T(1,128)} %param.20) | copy-start | bytes 3076
  204.6 43.0 %copy-start.3 = (s32[1024]{0:T(1024)S(1)}, s32[1024]{0:T(1024)}, u32[]{:S(2)}) copy-start(s32[1024]{0:T(1024)} %param.16) | copy-start | bytes 12292
  204.6 61.0 %copy-start.5 = (s32[1,256]{1,0:T(1,128)S(1)}, s32[1,256]{1,0:T(1,128)}, u32[]{:S(2)}) copy-start(s32[1,256]{1,0:T(1,128)} %param.18) | copy-start | bytes 3076
  204.6 111.9 %copy-start.2 = (bf16[1024,256]{1,0:T(8,128)(2,1)S(1)}, bf16[1024,256]{1,0:T(8,128)(2,1)}, u32[]{:S(2)}) copy-start(bf16[1024,256]{1,0:T(8,128)(2,1)} %param.15) | copy-start | bytes 1572868
  242.7 12.6 %all-to-all-start.2 = ((s32[32,1,32]{2,1,0:T(1,128)}), s32[32,1,32]{2,1,0:T(1,128)S(1)}, u32[]{:S(2)}, u32[]{:S(2)}) async-start(s32[32,1,32]{2,1,0:T(1,128)} %broadcast_in_dim.52), calls=%async_computation.2 | async-start | bytes 32768 | tf_op jit(solution)/shard_map/all_to_all | solution.py:51
  257.8 54.7 %all-to-all-start.3 = ((s32[32,1,16]{2,1,0:T(1,128)}), s32[32,1,16]{2,1,0:T(1,128)S(1)}, u32[]{:S(2)}, u32[]{:S(2)}) async-start(s32[32,1,16]{2,1,0:T(1,128)} %bitcast.38), calls=%async_computation.3 | async-start | bytes 32768 | tf_op jit(solution)/shard_map/all_to_all | solution.py:186
  312.5 71.9 %all-to-all-start.4 = ((bf16[32,16,256]{2,1,0:T(8,128)(2,1)}), bf16[32,16,256]{2,1,0:T(8,128)(2,1)S(1)}, u32[]{:S(2)}, u32[]{:S(2)}) async-start(bf16[32,16,256]{2,1,0:T(8,128)(2,1)} %bitcast.41), calls=%async_computation.4 | async-start | bytes 524288 | tf_op jit(solution)/shard_map/all_to_all | solution.py:179
  387.0 0.8 copy-start.1
Sparse Core Ops, SparseCore 0:
  242.1 60.3 all-gather.6
